TPU v7x, 128 devices: a whole 4x4x4 slice. The times are simulated.
128 devices in a mesh: front: 4 (over z), tile: 32 (over x, y, core).
Axes of the slice: x: 4, y: 4, z: 4, core: 2. Of those that a mesh axis runs over, the one named last changes fastest.
Arguments:
- front_entries: float32 [4, 4096, 4096], P('front', 'tile')
- child_blocks: bfloat16 [512, 64, 256], P(('front', 'tile'))
- child_map: int32 [128, 256], replicated, may hold values from -1 to 4095, as said below
- parent_list: int32 [128, 1], replicated, may hold values from 0 to 3; in each aligned block of 4 rows (0 to 3, 4 to 7, ...) at most 2 rows name the same one
Outputs:
- front_out: float32 [4, 4096, 4096], P('front', 'tile')
Inputs may be any that keep to these rules, and one draw needn't show every extreme that they name: `child_map`: row c gives the parent-front row of each of the 256 rows of child c: live entries come first and are distinct, -1 marks padding, every row has 128 to 256 live entries, and its first entry is 4095. `parent_list`: in each aligned block of 4 rows no front is named more than 2 times.
All inputs are finite; a program needn't handle non-finite values.
Results may differ from a plain program's by a relative error of at most 0.0003.
Values may be sent and summed in bfloat16 or wider, within the bound.
A program may use at most 128 MiB of HBM per device.

v0:
```python
import jax
import jax.numpy as jnp
from jax import lax
from jax.sharding import PartitionSpec as P

FRONT = 4096
PANEL = 512
PANELS = 2
CHILD = 256
BLOCK_ROWS = 64
BLK_DEV = 4
CAPACITY = 2


def routing(child_map, parent_list, front_count, tile_count, group_id):
    child_count = child_map.shape[0]
    fronts = jnp.arange(front_count, dtype=jnp.int32)
    target = parent_list[:, 0]
    blocks = (
        jnp.arange(front_count * tile_count, dtype=jnp.int32)[:, None] * BLK_DEV
        + jnp.arange(BLK_DEV, dtype=jnp.int32)[None, :]
    )
    child_of = blocks % child_count
    part_of = blocks // child_count
    child_ids = jnp.arange(child_count, dtype=jnp.int32)
    dest_front = jnp.sum(jnp.where(child_of[..., None] == child_ids, target, 0), axis=2)
    earlier = jnp.arange(BLK_DEV)[:, None] > jnp.arange(BLK_DEV)[None, :]
    same_dest = dest_front[:, :, None] == dest_front[:, None, :]
    slot_rank = jnp.sum(same_dest & earlier[None], axis=2)
    slot_ids = jnp.arange(CAPACITY, dtype=jnp.int32)
    select = (dest_front[:, None, None, :] == fronts[None, :, None, None]) & (
        slot_rank[:, None, None, :] == slot_ids[None, None, :, None]
    )
    to_group = select[:, group_id]
    slot_live = jnp.any(to_group, axis=2)
    slot_child = jnp.sum(jnp.where(to_group, child_of[:, None, :], 0), axis=2)
    slot_part = jnp.sum(jnp.where(to_group, part_of[:, None, :], 0), axis=2)
    return (select, slot_live, slot_child, slot_part)


def body(front_entries, child_blocks, child_map, parent_list):
    tile_count = lax.axis_size("tile")
    front_count = lax.axis_size("front")
    group_id = lax.axis_index("front")
    tile_id = lax.axis_index("tile")
    rows_dev = front_entries.shape[1]
    first_row = tile_id * rows_dev
    child_count = child_map.shape[0]
    select, slot_live, slot_child, slot_part = routing(
        child_map, parent_list, front_count, tile_count, group_id
    )
    self_dev = group_id * tile_count + tile_id
    own_select = select[self_dev].astype(jnp.bfloat16)
    outgoing = jnp.einsum(
        "dsj,jrk->dsrk", own_select, child_blocks, preferred_element_type=jnp.float32
    ).astype(jnp.bfloat16)
    incoming = lax.all_to_all(outgoing, "front", split_axis=0, concat_axis=0, tiled=True)
    child_hot = (slot_child[..., None] == jnp.arange(child_count, dtype=jnp.int32)).astype(
        jnp.float32
    )
    map_values = jnp.einsum(
        "dsn,nk->dsk", child_hot, child_map.astype(jnp.float32), precision=lax.Precision.HIGHEST
    )
    col_flat = map_values.astype(jnp.int32)
    part_count = CHILD // BLOCK_ROWS
    col_parts = col_flat.reshape(col_flat.shape[0], CAPACITY, part_count, BLOCK_ROWS)
    part_hot = slot_part[..., None] == jnp.arange(part_count, dtype=jnp.int32)
    row_maps = jnp.sum(jnp.where(part_hot[..., None], col_parts, 0), axis=2)
    row_valid = slot_live[..., None] & (row_maps >= 0)
    row_table = jnp.where(row_valid, row_maps, FRONT).reshape(
        front_count, tile_count, CAPACITY, BLOCK_ROWS
    )
    col_table = col_flat.reshape(front_count, tile_count, CAPACITY, CHILD)
    empty_cols = jnp.zeros((FRONT, rows_dev), jnp.float32)
    front_ids = jnp.arange(FRONT, dtype=jnp.int32)
    own_columns = first_row + jnp.arange(rows_dev)
    shards = lax.all_gather(incoming[None], "tile", axis=0, tiled=True)

    def one_tile(tile_step, running):
        child_rows = lax.dynamic_index_in_dim(shards, tile_step, 0, keepdims=False)
        col_maps = lax.dynamic_index_in_dim(col_table, tile_step, 1, keepdims=False)
        matches = (col_maps[..., None] == own_columns[None, None, None, :]).astype(jnp.bfloat16)
        values = jnp.einsum(
            "gsrk,gskc->gsrc", child_rows, matches, preferred_element_type=jnp.float32
        ).astype(jnp.bfloat16)
        targets = lax.dynamic_index_in_dim(row_table, tile_step, 1, keepdims=False)
        row_hot = (targets[..., None] == front_ids).astype(jnp.bfloat16)
        return running + jnp.einsum(
            "gsrf,gsrc->fc", row_hot, values, preferred_element_type=jnp.float32
        )

    extend_cols = lax.fori_loop(0, shards.shape[0], one_tile, empty_cols)
    matrix = front_entries[0] + extend_cols.T
    row_ids = first_row + jnp.arange(rows_dev)
    for panel_no in range(PANELS):
        left_col = panel_no * PANEL
        right_col = left_col + PANEL
        cols_piece = matrix[:, left_col:right_col]
        gathered = lax.all_gather(
            cols_piece.astype(jnp.bfloat16), "tile", axis=0, tiled=True
        ).astype(cols_piece.dtype)
        diag_factor = jnp.linalg.cholesky(gathered[left_col:right_col])
        lower_part = jax.scipy.linalg.solve_triangular(
            diag_factor, gathered[right_col:].T, lower=True
        ).T
        factor = jnp.concatenate([diag_factor, lower_part], 0)
        slice_start = jnp.clip(first_row - left_col, 0, FRONT - left_col - rows_dev)
        own_rows = lax.dynamic_slice_in_dim(factor, slice_start, rows_dev, 0)
        trailing = jnp.where((row_ids >= right_col)[:, None], own_rows, 0.0)
        remainder = matrix[:, right_col:] - jnp.dot(
            trailing, lower_part.T, precision=lax.Precision.HIGHEST
        )
        in_lower = row_ids[:, None] - left_col >= jnp.arange(PANEL)[None, :]
        panel_out = jnp.where(in_lower, own_rows, cols_piece)
        matrix = jnp.concatenate([matrix[:, :left_col], panel_out, remainder], 1)
    return matrix[None]


def solution(mesh):
    return jax.shard_map(
        body,
        mesh=mesh,
        in_specs=(P("front", "tile", None), P(("front", "tile"), None, None), P(), P()),
        out_specs=P("front", "tile", None),
        check_vma=False,
    )
```

profile of v0, /device:TPU:1, one launch (start us, length us, event | category | flops | bytes accessed | tf_op | source)
XLA Modules:
  0.0 746.4 jit_solution(17177670713988524720)
XLA Ops:
  11.6 11.3 %all_to_all.5 = bf16[4,2,64,256]{3,2,1,0:T(8,128)(2,1)} all-to-all(bf16[4,2,64,256]{3,2,1,0:T(8,128)(2,1)S(1)} %copy.98), channel_id=1, replica_groups=mesh['front'=4,'tile'=32] {'front'}, dimensions={0} | all-to-all | bytes 524288 | tf_op jit(solution)/shard_map/all_to_all | solution.py:57
  30.5 46.6 %all-gather.9.cloned.1.call-done = bf16[128,2,64,256]{3,2,1,0:T(8,128)(2,1)} async-done(((bf16[4,2,64,256]{3,2,1,0:T(8,128)(2,1)}), bf16[128,2,64,256]{3,2,1,0:T(8,128)(2,1)}) %all-gather.9.cloned.1.call-update) | async-done | bytes 8388624 | tf_op jit(solution)/shard_map/all_gather | solution.py:77
  77.2 186.3 %while.18 = (s32[]{:T(128)}, f32[4096,128]{1,0:T(8,128)}, s32[4,32,2,64]{3,1,0,2:T(8,128)S(1)}, bf16[32,4,2,64,256]{4,3,2,1,0:T(8,128)(2,1)}, s32[4,32,2,256]{3,...) while((s32[]{:T(128)}, f32[4096,128]{1,0:T(8,128)}, s32[4,32,2,64]{3,1,0,2:T(8,128)S(1)}, ...), condition=%wide.region_7.8_spmd.clone, body=%wide.region_6.7_spmd.clone.sunk | while | flops 573898880 | bytes 4508791 | solution.py:92
  82.4 5.8 fusion.141
  94.1 5.8 fusion.141
  105.7 5.8 fusion.141
  111.6 5.8 fusion.141
  117.4 5.8 fusion.141
  123.3 5.8 fusion.141
  129.1 5.8 fusion.141
  135.0 5.8 fusion.141
  140.8 5.8 fusion.141
  146.6 5.8 fusion.141
  152.5 5.8 fusion.141
  158.3 5.8 fusion.141
  170.0 5.8 fusion.141
  181.7 5.8 fusion.141
  193.4 5.8 fusion.141
  205.1 5.8 fusion.141
  216.8 5.8 fusion.141
  222.6 5.8 fusion.141
  228.5 5.8 fusion.141
  234.3 5.8 fusion.141
  240.2 5.8 fusion.141
  246.0 5.8 fusion.141
  251.8 5.8 fusion.141
  267.6 48.6 %all-gather.5.cloned.1.call-done = bf16[4096,512]{0,1:T(8,128)(2,1)} async-done(((bf16[128,512]{0,1:T(8,128)(2,1)}), bf16[4096,512]{0,1:T(8,128)(2,1)}) %all-gather.5.cloned.1.call-update) | async-done | bytes 4194320 | tf_op jit(solution)/shard_map/all_gather | solution.py:99
  324.8 11.7 %cholesky.286 = f32[128,128]{1,0:T(8,128)S(1)} custom-call(f32[128,128]{1,0:T(8,128)S(1)} %cholesky.426), custom_call_target="Cholesky" | custom-call | tf_op jit(solution)/shard_map/jit(cholesky)/cholesky | solution.py:102
  336.7 9.8 %custom-call.34 = f32[1,128,128]{1,2,0:T(8,128)S(1)} custom-call(f32[1,128,128]{2,1,0:T(8,128)S(1)} %get-tuple-element.280), custom_call_target="InvertDiagBlocksLowerTriangular" | custom-call | tf_op jit(solution)/shard_map/jit(cholesky)/cholesky | solution.py:102
  347.3 12.1 %cholesky.305 = f32[128,128]{1,0:T(8,128)S(1)} custom-call(f32[128,128]{1,0:T(8,128)S(1)} %cholesky.430), custom_call_target="Cholesky" | custom-call | tf_op jit(solution)/shard_map/jit(cholesky)/cholesky | solution.py:102
  359.6 9.8 %custom-call.35 = f32[1,128,128]{1,2,0:T(8,128)S(1)} custom-call(f32[1,128,128]{2,1,0:T(8,128)S(1)} %get-tuple-element.278), custom_call_target="InvertDiagBlocksLowerTriangular" | custom-call | tf_op jit(solution)/shard_map/jit(cholesky)/cholesky | solution.py:102
  374.4 11.7 %cholesky.326 = f32[128,128]{1,0:T(8,128)S(1)} custom-call(f32[128,128]{1,0:T(8,128)S(1)} %cholesky.435), custom_call_target="Cholesky" | custom-call | tf_op jit(solution)/shard_map/jit(cholesky)/cholesky | solution.py:102
  386.9 9.8 %custom-call.36 = f32[1,128,128]{1,2,0:T(8,128)S(1)} custom-call(f32[1,128,128]{2,1,0:T(8,128)S(1)} %get-tuple-element.276), custom_call_target="InvertDiagBlocksLowerTriangular" | custom-call | tf_op jit(solution)/shard_map/jit(cholesky)/cholesky | solution.py:102
  399.1 11.9 %cholesky.343 = f32[128,128]{1,0:T(8,128)S(1)} custom-call(f32[128,128]{1,0:T(8,128)S(1)} %convolution_subtract_fusion.11), custom_call_target="Cholesky" | custom-call | tf_op jit(solution)/shard_map/jit(cholesky)/cholesky | solution.py:102
  419.5 11.4 %while.16 = (s32[]{:T(128)}, f32[512,512]{0,1:T(8,128)}, s32[4,2]{0,1:T(2,128)S(1)}, f32[4,128,128]{2,1,0:T(8,128)S(1)}, s32[]{:T(128)}) while((s32[]{:T(128)}, f32[512,512]{0,1:T(8,128)}, s32[4,2]{0,1:T(2,128)S(1)}, f32[4,128,128]{2,1,0:T(8,128)S(1)}, s32[]{:T(128)}) %tuple.89), condition=%wide.while_cond, body=%wide.while_body.sunk | while | flops 2 | bytes 393329 | solution.py:103
  431.6 40.1 %custom-call.28 = f32[4,128,128]{1,2,0:T(8,128)S(1)} custom-call(f32[4,128,128]{2,1,0:T(8,128)} %copy-done.8), custom_call_target="InvertDiagBlocksLowerTriangular" | custom-call | tf_op jit(solution)/shard_map/jit(_solve_triangular)/triangular_solve | solution.py:103
  493.7 12.4 %convolution_subtract_fusion = f32[128,3584]{0,1:T(8,128)S(1)} fusion(f32[128,3584]{1,0:T(8,128)S(1)} %fusion.90, f32[128,3584]{1,0:T(8,128)S(1)} %fusion.91, f32[128,3584]{1,0:T(8,128)S(1)} %fusion.93, f32[128,3584]{1,0:T(8,128)S(1)} %fusion.50, f32[128,4096]{0,1:T(8,128)S(1)} %copy-done.3, pred[128]{0:T(512)(128)(4,1)S(1)} %broadcast_compare_fusion.1, ...), kind=kOutput, calls=%fused_computation.37 | convolution fusion | flops 2824667136 | bytes 19398788 | tf_op jit(solution)/shard_map/dot_general | solution.py:110
  508.2 48.6 %all-gather.7.cloned.1.call-done = bf16[4096,512]{0,1:T(8,128)(2,1)} async-done(((bf16[128,512]{0,1:T(8,128)(2,1)}), bf16[4096,512]{0,1:T(8,128)(2,1)}) %all-gather.7.cloned.1.call-update) | async-done | bytes 4194320 | tf_op jit(solution)/shard_map/all_gather | solution.py:99
  564.9 11.7 %cholesky.358 = f32[128,128]{1,0:T(8,128)S(1)} custom-call(f32[128,128]{1,0:T(8,128)S(1)} %cholesky.439), custom_call_target="Cholesky" | custom-call | tf_op jit(solution)/shard_map/jit(cholesky)/cholesky | solution.py:102
  576.8 9.8 %custom-call.37 = f32[1,128,128]{1,2,0:T(8,128)S(1)} custom-call(f32[1,128,128]{2,1,0:T(8,128)S(1)} %get-tuple-element.274), custom_call_target="InvertDiagBlocksLowerTriangular" | custom-call | tf_op jit(solution)/shard_map/jit(cholesky)/cholesky | solution.py:102
  587.4 12.1 %cholesky.377 = f32[128,128]{1,0:T(8,128)S(1)} custom-call(f32[128,128]{1,0:T(8,128)S(1)} %cholesky.443), custom_call_target="Cholesky" | custom-call | tf_op jit(solution)/shard_map/jit(cholesky)/cholesky | solution.py:102
  599.6 9.8 %custom-call.38 = f32[1,128,128]{1,2,0:T(8,128)S(1)} custom-call(f32[1,128,128]{2,1,0:T(8,128)S(1)} %get-tuple-element.272), custom_call_target="InvertDiagBlocksLowerTriangular" | custom-call | tf_op jit(solution)/shard_map/jit(cholesky)/cholesky | solution.py:102
  610.5 11.7 %cholesky.398 = f32[128,128]{1,0:T(8,128)S(1)} custom-call(f32[128,128]{1,0:T(8,128)S(1)} %cholesky.448), custom_call_target="Cholesky" | custom-call | tf_op jit(solution)/shard_map/jit(cholesky)/cholesky | solution.py:102
  622.4 9.8 %custom-call.39 = f32[1,128,128]{1,2,0:T(8,128)S(1)} custom-call(f32[1,128,128]{2,1,0:T(8,128)S(1)} %get-tuple-element.270), custom_call_target="InvertDiagBlocksLowerTriangular" | custom-call | tf_op jit(solution)/shard_map/jit(cholesky)/cholesky | solution.py:102
  633.0 11.9 %cholesky.415 = f32[128,128]{1,0:T(8,128)S(1)} custom-call(f32[128,128]{1,0:T(8,128)S(1)} %convolution_subtract_fusion.10), custom_call_target="Cholesky" | custom-call | tf_op jit(solution)/shard_map/jit(cholesky)/cholesky | solution.py:102
  653.5 14.5 %while.17 = (s32[]{:T(128)}, f32[512,512]{0,1:T(8,128)}, s32[4,2]{0,1:T(2,128)S(1)}, f32[4,128,128]{2,1,0:T(8,128)}, s32[]{:T(128)}) while((s32[]{:T(128)}, f32[512,512]{0,1:T(8,128)}, s32[4,2]{0,1:T(2,128)S(1)}, f32[4,128,128]{2,1,0:T(8,128)}, s32[]{:T(128)}) %tuple.102), condition=%wide.while_cond.1, body=%wide.while_body.1.sunk | while | flops 2 | bytes 393329 | solution.py:103
  668.0 40.7 %custom-call.29 = f32[4,128,128]{1,2,0:T(8,128)} custom-call(f32[4,128,128]{2,1,0:T(8,128)} %get-tuple-element.146), custom_call_target="InvertDiagBlocksLowerTriangular" | custom-call | tf_op jit(solution)/shard_map/jit(_solve_triangular)/triangular_solve | solution.py:103
  726.9 10.5 %convolution_subtract_fusion.4 = f32[128,3072]{0,1:T(8,128)S(1)} fusion(f32[128,3072]{1,0:T(8,128)S(1)} %fusion.84, f32[128,3072]{1,0:T(8,128)S(1)} %fusion.85, f32[128,3072]{1,0:T(8,128)S(1)} %fusion.87, f32[128,3072]{1,0:T(8,128)S(1)} %fusion.52, f32[128,3584]{0,1:T(8,128)S(1)} %copy-done.5, pred[128]{0:T(512)(128)(4,1)S(1)} %broadcast_compare_fusion, ...), kind=kOutput, calls=%fused_computation.49 | convolution fusion | flops 2421161984 | bytes 16777348 | tf_op jit(solution)/shard_map/dot_general | solution.py:110
  (365 shorter events, 180.6 us)
Async XLA Ops:
  6.5 21.4 %copy-start.9 = (s32[128,256]{1,0:T(8,128)S(1)}, s32[128,256]{1,0:T(8,128)}, u32[]{:S(2)}) copy-start(s32[128,256]{1,0:T(8,128)} %param.9) | copy-start | bytes 393220
  6.5 70.7 %all-gather.9.cloned.1.call-start = ((), (), s32[]{:S(2)}) async-start(), calls=%async_computation.3 | async-start | bytes 8650752 | tf_op jit(solution)/shard_map/all_gather | solution.py:77
  22.9 293.2 %all-gather.5.cloned.1.call-start = ((), (), s32[]{:S(2)}) async-start(), calls=%async_computation.1 | async-start | bytes 4325376 | tf_op jit(solution)/shard_map/all_gather | solution.py:99
  265.3 1.3 copy-start.2
  267.3 289.5 %all-gather.7.cloned.1.call-start = ((), (), s32[]{:S(2)}) async-start(), calls=%async_computation.2 | async-start | bytes 4325376 | tf_op jit(solution)/shard_map/all_gather | solution.py:99
  416.4 58.7 %slice-start = ((s8[7340032]{0:T(1024)(128)(4,1)}), s8[3145728]{0:T(1024)(128)(4,1)S(1)}, s32[]{:S(2)}) async-start(s8[7340032]{0:T(1024)(128)(4,1)} %bitcast.155), calls=%async_computation.4 | async-start | bytes 6291456
  430.9 0.7 copy-start.8
  471.7 3.4 slice-start.1
  490.8 1.2 copy-start.1
  490.8 2.8 copy-start.3
  491.4 14.7 %copy-start = (f32[3584,512]{0,1:T(8,128)}, f32[3584,512]{0,1:T(8,128)S(1)}, u32[]{:S(2)}) copy-start(f32[3584,512]{0,1:T(8,128)S(1)} %fusion.35) | copy-start | bytes 22020100
  506.0 1.2 copy-start.4
  647.6 1.9 copy-start.6
  650.1 61.7 %slice-start.2 = ((s8[6291456]{0:T(1024)(128)(4,1)}), s8[2097152]{0:T(1024)(128)(4,1)S(1)}, s32[]{:S(2)}) async-start(s8[6291456]{0:T(1024)(128)(4,1)} %bitcast.157), calls=%async_computation.6 | async-start | bytes 4194304
  708.7 2.3 copy-start.7
  708.7 3.2 slice-start.3
  725.4 1.5 copy-start.5
Sparse Core Ops, SparseCore 0:
  23.1 54.0 all-gather.8
  267.4 48.7 all-gather.4
  508.1 48.6 all-gather.6
where the time goes:
time: 756 us; the launch traced here: 746 us
  other arithmetic  265 us (35%)
  matrix products  247 us (33%)
  waiting for transfers between devices  144 us (19%)
  local copies, waits for them, and re-layouts  58.7 us (8%)
  between operations  19.3 us (3%)
  blocking collectives  11.3 us (1%)
    dot_general x32, matrix products, one_tile(): jnp.einsum('gsrf,gsrc->fc', row_hot, values, preferred_element_type=jnp.f...  184 us
    another operation x29, other arithmetic, body(): diag_factor = jnp.linalg.cholesky(gathered[left_col:right_col])  159 us
    all_gather x2, waiting for transfers between devices, body(): lax.all_gather(cols_piece.astype(jnp.bfloat16), 'tile', axis=0, tiled=True)  97.2 us
    another operation x5, other arithmetic, body(): jax.scipy.linalg.solve_triangular(diag_factor, gathered[right_col:].T, lo...  86.6 us
    all_gather x1, waiting for transfers between devices, body(): shards = lax.all_gather(incoming[None], 'tile', axis=0, tiled=True)  46.6 us
    another operation x14, matrix products, body(): jax.scipy.linalg.solve_triangular(diag_factor, gathered[right_col:].T, lo...  30.7 us
    another operation x40, local copies, waits for them, and re-layouts  25.7 us
    dot_general x2, matrix products, body(): jnp.dot(trailing, lower_part.T, precision=lax.Precision.HIGHEST)  22.8 us
  transfers between devices with their start and end apart: 3, of which 3 were waited for; matrix products, arithmetic and copies ran while one was open for 1% of the time, Pallas kernels for 0%

commit v1 on v0

--- a/solution.py
+++ b/solution.py
@@ -74,7 +74,9 @@
     empty_cols = jnp.zeros((FRONT, rows_dev), jnp.float32)
     front_ids = jnp.arange(FRONT, dtype=jnp.int32)
     own_columns = first_row + jnp.arange(rows_dev)
-    shards = lax.all_gather(incoming[None], "tile", axis=0, tiled=True)
+    shards = jnp.concatenate(
+        lax.all_to_all(jnp.stack([incoming[None]] * lax.axis_size("tile")), "tile", 0, 0), axis=0
+    )
 
     def one_tile(tile_step, running):
         child_rows = lax.dynamic_index_in_dim(shards, tile_step, 0, keepdims=False)

time: 756 us -> 846 us (1.12)
  waiting for transfers between devices: 144 us -> 212 us
  local copies, waits for them, and re-layouts: 58.7 us -> 72.9 us
  starting transfers between devices: 0.3 us -> 9.65 us
    all_to_all x0 -> x1, waiting for transfers between devices: none -> 101 us  [body(): lax.all_to_all(jnp.stack([incoming[None]] * lax.axis_size('tile')), 'tile...]
    all_gather x1 -> x0, waiting for transfers between devices: 46.6 us -> none  [body(): shards = lax.all_gather(incoming[None], 'tile', axis=0, tiled=True)]
    all_gather x2, waiting for transfers between devices: 97.2 us -> 111 us  [body(): lax.all_gather(cols_piece.astype(jnp.bfloat16), 'tile', axis=0, tiled=True)]
    all_to_all x0 -> x1, starting transfers between devices: none -> 9.35 us  [body(): lax.all_to_all(jnp.stack([incoming[None]] * lax.axis_size('tile')), 'tile...]
    another operation x40 -> x41, local copies, waits for them, and re-layouts: 25.7 us -> 30.5 us
where the time goes in v1:
time: 846 us; the launch traced here: 835 us
  other arithmetic  264 us (31%)
  matrix products  244 us (29%)
  waiting for transfers between devices  212 us (25%)
  local copies, waits for them, and re-layouts  72.9 us (9%)
  between operations  19.7 us (2%)
  blocking collectives  11.2 us (1%)
  starting transfers between devices  9.65 us (1%)
    dot_general x32, matrix products, one_tile(): jnp.einsum('gsrf,gsrc->fc', row_hot, values, preferred_element_type=jnp.f...  184 us
    another operation x29, other arithmetic, body(): diag_factor = jnp.linalg.cholesky(gathered[left_col:right_col])  158 us
    all_gather x2, waiting for transfers between devices, body(): lax.all_gather(cols_piece.astype(jnp.bfloat16), 'tile', axis=0, tiled=True)  111 us
    all_to_all x1, waiting for transfers between devices, body(): lax.all_to_all(jnp.stack([incoming[None]] * lax.axis_size('tile')), 'tile...  101 us
    another operation x5, other arithmetic, body(): jax.scipy.linalg.solve_triangular(diag_factor, gathered[right_col:].T, lo...  86.5 us
    another operation x14, matrix products, body(): jax.scipy.linalg.solve_triangular(diag_factor, gathered[right_col:].T, lo...  30.7 us
    another operation x40, local copies, waits for them, and re-layouts  26.2 us
    dot_general x2, matrix products, body(): jnp.dot(trailing, lower_part.T, precision=lax.Precision.HIGHEST)  22.8 us
  transfers between devices with their start and end apart: 3, of which 3 were waited for; matrix products, arithmetic and copies ran while one was open for 1% of the time, Pallas kernels for 0%

profile of v1, /device:TPU:1, one launch (start us, length us, event | category | flops | bytes accessed | tf_op | source)
XLA Modules:
  0.0 835.2 jit_solution(9615403740856751535)
XLA Ops:
  11.5 11.2 %all_to_all.10 = bf16[4,2,64,256]{3,2,1,0:T(8,128)(2,1)S(1)} all-to-all(bf16[4,2,64,256]{3,2,1,0:T(8,128)(2,1)S(1)} %copy.98), channel_id=1, replica_groups=mesh['front'=4,'tile'=32] {'front'}, dimensions={0} | all-to-all | bytes 524288 | tf_op jit(solution)/shard_map/all_to_all | solution.py:57
  27.0 9.3 %all-to-all-start.1 = ((bf16[32,1,4,2,64,256]{5,4,3,2,1,0:T(8,128)(2,1)}), bf16[32,1,4,2,64,256]{5,4,3,2,1,0:T(8,128)(2,1)}, u32[]{:S(2)}, u32[]{:S(2)}) async-start(bf16[32,1,4,2,64,256]{5,4,3,2,1,0:T(8,128)(2,1)} %stack.3), calls=%async_computation.1 | async-start | bytes 16777216 | tf_op jit(solution)/shard_map/all_to_all | solution.py:78
  44.0 100.9 %all-to-all-done.1 = bf16[32,1,4,2,64,256]{5,4,3,2,1,0:T(8,128)(2,1)} async-done(((bf16[32,1,4,2,64,256]{5,4,3,2,1,0:T(8,128)(2,1)}), bf16[32,1,4,2,64,256]{5,4,3,2,1,0:T(8,128)(2,1)}, u32[]{:S(2)}, u32[]{:S(2)}) %all-to-all-start.1) | async-done | bytes 8388640 | tf_op jit(solution)/shard_map/all_to_all | solution.py:78
  144.9 186.7 %while.18 = (s32[]{:T(128)}, f32[4096,128]{1,0:T(8,128)}, s32[4,32,2,64]{3,1,0,2:T(8,128)S(1)}, bf16[32,4,2,64,256]{4,3,2,1,0:T(8,128)(2,1)}, s32[4,32,2,256]{3,...) while((s32[]{:T(128)}, f32[4096,128]{1,0:T(8,128)}, s32[4,32,2,64]{3,1,0,2:T(8,128)S(1)}, ...), condition=%wide.region_7.8_spmd.clone, body=%wide.region_6.7_spmd.clone.sunk | while | flops 573898880 | bytes 4509291 | solution.py:94
  150.1 5.8 fusion.141
  179.4 5.8 fusion.141
  185.3 5.8 fusion.141
  191.1 5.8 fusion.141
  197.0 5.8 fusion.141
  202.8 5.8 fusion.141
  220.4 5.8 fusion.141
  226.3 5.8 fusion.141
  232.1 5.8 fusion.141
  238.0 5.8 fusion.141
  243.8 5.8 fusion.141
  249.7 5.8 fusion.141
  255.6 5.8 fusion.141
  279.0 5.8 fusion.141
  284.8 5.8 fusion.141
  290.7 5.8 fusion.141
  296.6 5.8 fusion.141
  302.4 5.8 fusion.141
  308.3 5.8 fusion.141
  314.1 5.8 fusion.141
  335.7 62.6 %all-gather.3.cloned.1.call-done = bf16[4096,512]{0,1:T(8,128)(2,1)} async-done(((bf16[128,512]{0,1:T(8,128)(2,1)}), bf16[4096,512]{0,1:T(8,128)(2,1)}) %all-gather.3.cloned.1.call-update) | async-done | bytes 4194320 | tf_op jit(solution)/shard_map/all_gather | solution.py:101
  406.5 11.7 %cholesky.286 = f32[128,128]{1,0:T(8,128)S(1)} custom-call(f32[128,128]{1,0:T(8,128)S(1)} %cholesky.426), custom_call_target="Cholesky" | custom-call | tf_op jit(solution)/shard_map/jit(cholesky)/cholesky | solution.py:104
  418.3 9.8 %custom-call.34 = f32[1,128,128]{1,2,0:T(8,128)S(1)} custom-call(f32[1,128,128]{2,1,0:T(8,128)S(1)} %get-tuple-element.280), custom_call_target="InvertDiagBlocksLowerTriangular" | custom-call | tf_op jit(solution)/shard_map/jit(cholesky)/cholesky | solution.py:104
  428.8 11.7 %cholesky.305 = f32[128,128]{1,0:T(8,128)S(1)} custom-call(f32[128,128]{1,0:T(8,128)S(1)} %cholesky.430), custom_call_target="Cholesky" | custom-call | tf_op jit(solution)/shard_map/jit(cholesky)/cholesky | solution.py:104
  440.9 10.2 %custom-call.35 = f32[1,128,128]{1,2,0:T(8,128)S(1)} custom-call(f32[1,128,128]{2,1,0:T(8,128)S(1)} %get-tuple-element.278), custom_call_target="InvertDiagBlocksLowerTriangular" | custom-call | tf_op jit(solution)/shard_map/jit(cholesky)/cholesky | solution.py:104
  452.2 11.7 %cholesky.326 = f32[128,128]{1,0:T(8,128)S(1)} custom-call(f32[128,128]{1,0:T(8,128)S(1)} %cholesky.435), custom_call_target="Cholesky" | custom-call | tf_op jit(solution)/shard_map/jit(cholesky)/cholesky | solution.py:104
  464.1 9.8 %custom-call.36 = f32[1,128,128]{1,2,0:T(8,128)S(1)} custom-call(f32[1,128,128]{2,1,0:T(8,128)S(1)} %get-tuple-element.276), custom_call_target="InvertDiagBlocksLowerTriangular" | custom-call | tf_op jit(solution)/shard_map/jit(cholesky)/cholesky | solution.py:104
  474.7 11.9 %cholesky.343 = f32[128,128]{1,0:T(8,128)S(1)} custom-call(f32[128,128]{1,0:T(8,128)S(1)} %convolution_subtract_fusion.11), custom_call_target="Cholesky" | custom-call | tf_op jit(solution)/shard_map/jit(cholesky)/cholesky | solution.py:104
  486.7 6.6 slice_bitcast_fusion
  501.0 12.2 %while.16 = (s32[]{:T(128)}, f32[512,512]{0,1:T(8,128)}, s32[4,2]{0,1:T(2,128)S(1)}, f32[4,128,128]{2,1,0:T(8,128)S(1)}, s32[]{:T(128)}) while((s32[]{:T(128)}, f32[512,512]{0,1:T(8,128)}, s32[4,2]{0,1:T(2,128)S(1)}, f32[4,128,128]{2,1,0:T(8,128)S(1)}, s32[]{:T(128)}) %tuple.89), condition=%wide.while_cond, body=%wide.while_body.sunk | while | flops 2 | bytes 393321 | solution.py:105
  513.8 40.1 %custom-call.28 = f32[4,128,128]{1,2,0:T(8,128)S(1)} custom-call(f32[4,128,128]{2,1,0:T(8,128)} %copy-done.11), custom_call_target="InvertDiagBlocksLowerTriangular" | custom-call | tf_op jit(solution)/shard_map/jit(_solve_triangular)/triangular_solve | solution.py:105
  575.9 12.4 %convolution_subtract_fusion = f32[128,3584]{0,1:T(8,128)S(1)} fusion(f32[128,3584]{1,0:T(8,128)S(1)} %fusion.90, f32[128,3584]{1,0:T(8,128)S(1)} %fusion.91, f32[128,3584]{1,0:T(8,128)S(1)} %fusion.93, f32[128,3584]{1,0:T(8,128)S(1)} %fusion.50, f32[128,4096]{0,1:T(8,128)S(1)} %copy-done.5, pred[128]{0:T(512)(128)(4,1)S(1)} %broadcast_compare_fusion.1, ...), kind=kOutput, calls=%fused_computation.37 | convolution fusion | flops 2824667136 | bytes 19398788 | tf_op jit(solution)/shard_map/dot_general | solution.py:112
  590.5 48.6 %all-gather.5.cloned.1.call-done = bf16[4096,512]{0,1:T(8,128)(2,1)} async-done(((bf16[128,512]{0,1:T(8,128)(2,1)}), bf16[4096,512]{0,1:T(8,128)(2,1)}) %all-gather.5.cloned.1.call-update) | async-done | bytes 4194320 | tf_op jit(solution)/shard_map/all_gather | solution.py:101
  647.3 11.7 %cholesky.358 = f32[128,128]{1,0:T(8,128)S(1)} custom-call(f32[128,128]{1,0:T(8,128)S(1)} %cholesky.439), custom_call_target="Cholesky" | custom-call | tf_op jit(solution)/shard_map/jit(cholesky)/cholesky | solution.py:104
  659.0 9.8 %custom-call.37 = f32[1,128,128]{1,2,0:T(8,128)S(1)} custom-call(f32[1,128,128]{2,1,0:T(8,128)S(1)} %get-tuple-element.274), custom_call_target="InvertDiagBlocksLowerTriangular" | custom-call | tf_op jit(solution)/shard_map/jit(cholesky)/cholesky | solution.py:104
  669.5 11.7 %cholesky.377 = f32[128,128]{1,0:T(8,128)S(1)} custom-call(f32[128,128]{1,0:T(8,128)S(1)} %cholesky.443), custom_call_target="Cholesky" | custom-call | tf_op jit(solution)/shard_map/jit(cholesky)/cholesky | solution.py:104
  682.0 9.8 %custom-call.38 = f32[1,128,128]{1,2,0:T(8,128)S(1)} custom-call(f32[1,128,128]{2,1,0:T(8,128)S(1)} %get-tuple-element.272), custom_call_target="InvertDiagBlocksLowerTriangular" | custom-call | tf_op jit(solution)/shard_map/jit(cholesky)/cholesky | solution.py:104
  692.9 11.7 %cholesky.398 = f32[128,128]{1,0:T(8,128)S(1)} custom-call(f32[128,128]{1,0:T(8,128)S(1)} %cholesky.448), custom_call_target="Cholesky" | custom-call | tf_op jit(solution)/shard_map/jit(cholesky)/cholesky | solution.py:104
  704.8 9.8 %custom-call.39 = f32[1,128,128]{1,2,0:T(8,128)S(1)} custom-call(f32[1,128,128]{2,1,0:T(8,128)S(1)} %get-tuple-element.270), custom_call_target="InvertDiagBlocksLowerTriangular" | custom-call | tf_op jit(solution)/shard_map/jit(cholesky)/cholesky | solution.py:104
  715.4 11.9 %cholesky.415 = f32[128,128]{1,0:T(8,128)S(1)} custom-call(f32[128,128]{1,0:T(8,128)S(1)} %convolution_subtract_fusion.10), custom_call_target="Cholesky" | custom-call | tf_op jit(solution)/shard_map/jit(cholesky)/cholesky | solution.py:104
  727.4 6.2 slice_bitcast_fusion.1
  742.3 14.2 %while.17 = (s32[]{:T(128)}, f32[512,512]{0,1:T(8,128)}, s32[4,2]{0,1:T(2,128)S(1)}, f32[4,128,128]{2,1,0:T(8,128)}, s32[]{:T(128)}) while((s32[]{:T(128)}, f32[512,512]{0,1:T(8,128)}, s32[4,2]{0,1:T(2,128)S(1)}, f32[4,128,128]{2,1,0:T(8,128)}, s32[]{:T(128)}) %tuple.100), condition=%wide.while_cond.1, body=%wide.while_body.1.sunk | while | flops 2 | bytes 393829 | solution.py:105
  756.5 40.7 %custom-call.29 = f32[4,128,128]{1,2,0:T(8,128)} custom-call(f32[4,128,128]{2,1,0:T(8,128)} %get-tuple-element.146), custom_call_target="InvertDiagBlocksLowerTriangular" | custom-call | tf_op jit(solution)/shard_map/jit(_solve_triangular)/triangular_solve | solution.py:105
  815.6 10.5 %convolution_subtract_fusion.4 = f32[128,3072]{0,1:T(8,128)S(1)} fusion(f32[128,3072]{1,0:T(8,128)S(1)} %fusion.84, f32[128,3072]{1,0:T(8,128)S(1)} %fusion.85, f32[128,3072]{1,0:T(8,128)S(1)} %fusion.87, f32[128,3072]{1,0:T(8,128)S(1)} %fusion.52, f32[128,3584]{0,1:T(8,128)S(1)} %copy-done.7, pred[128]{0:T(512)(128)(4,1)S(1)} %broadcast_compare_fusion, ...), kind=kOutput, calls=%fused_computation.49 | convolution fusion | flops 2421161984 | bytes 16777348 | tf_op jit(solution)/shard_map/dot_general | solution.py:112
  (371 shorter events, 196.1 us)
Async XLA Ops:
  27.0 14.2 %copy-start.12 = (s32[128,256]{1,0:T(8,128)S(1)}, s32[128,256]{1,0:T(8,128)}, u32[]{:S(2)}) copy-start(s32[128,256]{1,0:T(8,128)} %param.9) | copy-start | bytes 393220
  27.0 117.9 %all-to-all-start.1 = ((bf16[32,1,4,2,64,256]{5,4,3,2,1,0:T(8,128)(2,1)}), bf16[32,1,4,2,64,256]{5,4,3,2,1,0:T(8,128)(2,1)}, u32[]{:S(2)}, u32[]{:S(2)}) async-start(bf16[32,1,4,2,64,256]{5,4,3,2,1,0:T(8,128)(2,1)} %stack.3), calls=%async_computation.1 | async-start | bytes 16777216 | tf_op jit(solution)/shard_map/all_to_all | solution.py:78
  36.4 361.9 %all-gather.3.cloned.1.call-start = ((), (), s32[]{:S(2)}) async-start(), calls=%async_computation.2 | async-start | bytes 4325376 | tf_op jit(solution)/shard_map/all_gather | solution.py:101
  333.4 1.3 copy-start.4
  335.4 303.6 %all-gather.5.cloned.1.call-start = ((), (), s32[]{:S(2)}) async-start(), calls=%async_computation.3 | async-start | bytes 4325376 | tf_op jit(solution)/shard_map/all_gather | solution.py:101
  403.1 3.2 copy-start.1
  494.6 2.8 copy-start.8
  497.9 59.4 %slice-start = ((s8[7340032]{0:T(1024)(128)(4,1)}), s8[3145728]{0:T(1024)(128)(4,1)S(1)}, s32[]{:S(2)}) async-start(s8[7340032]{0:T(1024)(128)(4,1)} %bitcast.155), calls=%async_computation.4 | async-start | bytes 6291456
  513.1 0.7 copy-start.11
  554.0 3.4 slice-start.1
  573.0 1.2 copy-start.3
  573.1 2.8 copy-start.5
  573.6 14.7 %copy-start = (f32[3584,512]{0,1:T(8,128)}, f32[3584,512]{0,1:T(8,128)S(1)}, u32[]{:S(2)}) copy-start(f32[3584,512]{0,1:T(8,128)S(1)} %fusion.35) | copy-start | bytes 22020100
  588.3 1.2 copy-start.6
  643.8 3.2 copy-start.2
  736.3 1.9 copy-start.9
  738.9 61.4 %slice-start.2 = ((s8[6291456]{0:T(1024)(128)(4,1)}), s8[2097152]{0:T(1024)(128)(4,1)S(1)}, s32[]{:S(2)}) async-start(s8[6291456]{0:T(1024)(128)(4,1)} %bitcast.157), calls=%async_computation.6 | async-start | bytes 4194304
  797.2 2.3 copy-start.10
  797.2 3.2 slice-start.3
  813.9 1.5 copy-start.7
Sparse Core Ops, SparseCore 0:
  335.5 62.6 all-gather.2
  590.3 48.6 all-gather.4
